TPU v7x, 256 devices: a whole 4x4x8 slice. The times are simulated.
256 devices in a mesh: seq: 32 (over z_hi, x, core), fsdp: 8 (over z_lo, y).
Axes of the slice: x: 4, y: 4, z: 8 (z_hi: 4, z_lo: 2; z = z_hi * 2 + z_lo), core: 2. Of those that a mesh axis runs over, the one named last changes fastest.
Arguments:
- inputs: bfloat16 [8, 128, 32, 4096], P('fsdp', None, 'seq'), may hold values from -6 to 6
- queries: bfloat16 [8, 128, 32, 4096], P('fsdp', None, 'seq'), may hold values from -1000 to 1000
- rotated_keys: bfloat16 [8, 128, 32, 512], P('fsdp', None, 'seq'), may hold values from -6 to 6
- out_grad: bfloat16 [8, 128, 32, 4096], P('fsdp', None, 'seq'), may hold values from -6 to 6
- value_weight: bfloat16 [4096, 512], P(('seq', 'fsdp')), may hold values from -0.09375 to 0.09375
- fisher: float32 [4096, 512], P(('seq', 'fsdp')), may hold values from 0.2 to 20
- anchor: float32 [4096, 512], P(('seq', 'fsdp')), may hold values from -0.25 to 0.25
- doc_starts: int32 [8, 64], P('fsdp'), may hold values from 0 to 4064, as said below
- owners: int32 [8, 64], P('fsdp'), may hold values from 0 to 31, as said below
Outputs:
- query_grad: bfloat16 [8, 32, 6, 32, 4096], P('fsdp', 'seq')
- key_grad: bfloat16 [8, 128, 32, 512], P('fsdp', None, 'seq')
- input_grad: bfloat16 [8, 128, 32, 4096], P('fsdp', None, 'seq')
- ewc_grad: float32 [4096, 512], P(('seq', 'fsdp'))
Inputs may be any that keep to these rules, and one draw needn't show every extreme that they name: `doc_starts`: in each sequence the starts rise strictly from 0; every document's length (4096 minus the last start for the last one) is a multiple of 32. Each of the 32 owners is named by exactly two documents of a sequence; one owner's documents hold at most 192 positions in all, and in every sequence some owner holds exactly that many.
All inputs are finite; a program needn't handle non-finite values.
Results may differ from a plain program's by a relative error of at most 0.029.
Values may be sent and summed in bfloat16 or wider, within the bound.
No kernel may reach another device: no remote copies, remote signals or barrier semaphores. Data moves between devices by JAX's collectives and lax.ppermute only.
A program may use at most 128 MiB of HBM per device.

v0:
```python
import math
import jax
import jax.numpy as jnp
from jax import lax
from jax.sharding import PartitionSpec as P

KVH = 4
HD = 128
SCORE_NEG = -1e30
EWC_LAMBDA = 4.0


def round_plan(starts, owner_list, lane_count, rounds):
    round_ids = jnp.arange(rounds, dtype=jnp.int32)
    start_rounds = starts // lane_count
    doc_of = jnp.sum((start_rounds[None, :] <= round_ids[:, None]).astype(jnp.int32), axis=1) - 1
    doc_ids = jnp.arange(starts.shape[0], dtype=jnp.int32)
    onehot = (doc_of[:, None] == doc_ids[None, :]).astype(jnp.int32)
    owner_of = jnp.sum(onehot * owner_list[None, :], axis=1)
    earlier = (owner_of[:, None] == owner_of[None, :]) & (round_ids[None, :] < round_ids[:, None])
    rank_of = jnp.sum(earlier.astype(jnp.int32), axis=1)
    return (doc_of, owner_of, rank_of)


def slot_rounds(owner_of, rank_of, lane_count, capacity):
    lane_ids = jnp.arange(lane_count, dtype=jnp.int32)
    slot_ids = jnp.arange(capacity, dtype=jnp.int32)
    round_ids = jnp.arange(owner_of.shape[0], dtype=jnp.int32)
    match = (owner_of[None, None, :] == lane_ids[None, :, None]) & (
        rank_of[None, None, :] == slot_ids[:, None, None]
    )
    source = jnp.sum(match.astype(jnp.int32) * round_ids[None, None, :], axis=2)
    filled = jnp.any(match, axis=2)
    return (source, filled)


def attend(query_in, grad_in, key_in, value_in, visible):
    slot_count = query_in.shape[0] * query_in.shape[1]
    group = query_in.shape[3] // HD
    scale = 1.0 / math.sqrt(HD)
    query_parts = []
    key_parts = []
    value_parts = []
    for item_index in range(query_in.shape[2]):
        q_item = query_in[:, :, item_index, :].reshape(slot_count, group, HD)
        g_item = grad_in[:, :, item_index, :].reshape(slot_count, group, HD)
        k_item = key_in[:, :, item_index, :].reshape(slot_count, HD)
        v_item = value_in[:, :, item_index, :].reshape(slot_count, HD)
        scores = (
            jnp.einsum("mgd,kd->gmk", q_item, k_item, preferred_element_type=jnp.float32) * scale
        )
        masked = jnp.where(visible[None], scores, SCORE_NEG)
        peak = jnp.max(masked, axis=2, keepdims=True)
        probs = jnp.where(visible[None], jnp.exp(masked - peak), 0.0)
        totals = jnp.sum(probs, axis=2, keepdims=True)
        probs = probs / jnp.where(totals > 0.0, totals, 1.0)
        probs_b = probs.astype(jnp.bfloat16)
        attn_out = jnp.einsum(
            "gmk,kd->mgd", probs_b, v_item, preferred_element_type=jnp.float32
        ).astype(jnp.bfloat16)
        delta = jnp.einsum("mgd,mgd->gm", g_item, attn_out, preferred_element_type=jnp.float32)
        dprobs = jnp.einsum("mgd,kd->gmk", g_item, v_item, preferred_element_type=jnp.float32)
        dscores = (probs * (dprobs - delta[:, :, None]) * scale).astype(jnp.bfloat16)
        query_grad = jnp.einsum(
            "gmk,kd->mgd", dscores, k_item, preferred_element_type=jnp.float32
        ).astype(jnp.bfloat16)
        key_grad = jnp.einsum(
            "gmk,mgd->kd", dscores, q_item, preferred_element_type=jnp.float32
        ).astype(jnp.bfloat16)
        value_grad = jnp.einsum(
            "gmk,mgd->kd", probs_b, g_item, preferred_element_type=jnp.float32
        ).astype(jnp.bfloat16)
        query_parts.append(query_grad.reshape(query_in.shape[0], query_in.shape[1], group * HD))
        key_parts.append(key_grad.reshape(query_in.shape[0], query_in.shape[1], HD))
        value_parts.append(value_grad.reshape(query_in.shape[0], query_in.shape[1], HD))
    return (
        jnp.stack(query_parts, axis=2),
        jnp.stack(key_parts, axis=2),
        jnp.stack(value_parts, axis=2),
    )


def fetch_weight(value_weight):
    return lax.all_gather(value_weight, ("seq", "fsdp"), axis=0, tiled=True)


def body(inputs, queries, rotated_keys, out_grad, value_weight, fisher, anchor, doc_starts, owners):
    lane_count = lax.axis_size("seq")
    own_lane = lax.axis_index("seq")
    rounds = inputs.shape[1]
    capacity = 3 * rounds // (2 * lane_count)
    token_rows = inputs.reshape(rounds, inputs.shape[3])
    query_rows = queries.reshape(rounds, queries.shape[3])
    key_rows = rotated_keys.reshape(rounds, rotated_keys.shape[3])
    grad_rows = out_grad.reshape(rounds, out_grad.shape[3])
    doc_of, owner_of, rank_of = round_plan(doc_starts[0], owners[0], lane_count, rounds)
    source, filled = slot_rounds(owner_of, rank_of, lane_count, capacity)

    def to_slots(rows):
        picked = jnp.take(rows, source.reshape(-1), axis=0).reshape(capacity, lane_count, KVH, -1)
        return jnp.where(filled[:, :, None, None], picked, jnp.zeros_like(picked))

    query_send = to_slots(query_rows)
    grad_send = to_slots(grad_rows)
    key_send = to_slots(key_rows)
    my_rounds = lax.dynamic_index_in_dim(source, own_lane, 1, keepdims=False)
    my_filled = lax.dynamic_index_in_dim(filled, own_lane, 1, keepdims=False)
    lane_ids = jnp.arange(lane_count, dtype=jnp.int32)
    slot_pos = (my_rounds[:, None] * lane_count + lane_ids[None, :]).reshape(-1)
    round_doc = jnp.where(my_filled, jnp.take(doc_of, my_rounds), -1)
    slot_doc = jnp.broadcast_to(round_doc[:, None], (capacity, lane_count)).reshape(-1)
    slot_live = jnp.broadcast_to(my_filled[:, None], (capacity, lane_count)).reshape(-1)
    visible = (slot_doc[:, None] == slot_doc[None, :]) & (slot_pos[None, :] <= slot_pos[:, None])
    visible = visible & slot_live[:, None] & slot_live[None, :]
    full_weight = fetch_weight(value_weight)
    value_rows = jnp.dot(token_rows, full_weight, preferred_element_type=jnp.float32).astype(
        jnp.bfloat16
    )
    value_send = to_slots(value_rows)
    query_back, key_back, value_back = attend(
        lax.all_to_all(query_send, "seq", split_axis=1, concat_axis=1, tiled=True),
        lax.all_to_all(grad_send, "seq", split_axis=1, concat_axis=1, tiled=True),
        lax.all_to_all(key_send, "seq", split_axis=1, concat_axis=1, tiled=True),
        lax.all_to_all(value_send, "seq", split_axis=1, concat_axis=1, tiled=True),
        visible,
    )
    returned = (
        lax.all_to_all(key_back, "seq", split_axis=1, concat_axis=1, tiled=True),
        lax.all_to_all(value_back, "seq", split_axis=1, concat_axis=1, tiled=True),
    )
    flat_index = rank_of * lane_count + owner_of
    key_home = jnp.take(returned[0].reshape(capacity * lane_count, -1), flat_index, axis=0)
    value_home = jnp.take(returned[1].reshape(capacity * lane_count, -1), flat_index, axis=0)
    input_grad = jnp.einsum(
        "rk,dk->rd", value_home, full_weight, preferred_element_type=jnp.float32
    ).astype(jnp.bfloat16)
    partial_sum = jnp.einsum(
        "rd,rk->dk", token_rows, value_home, preferred_element_type=jnp.float32
    )
    summed = lax.psum_scatter(partial_sum, ("seq", "fsdp"), scatter_dimension=0, tiled=True)
    tokens_total = rounds * lane_count * lax.axis_size("fsdp")
    grad_scale = 1.0 / math.sqrt(tokens_total)
    ewc_grad = summed * grad_scale + EWC_LAMBDA * fisher * (
        value_weight.astype(jnp.float32) - anchor
    )
    query_out = query_back.reshape(1, 1, capacity, lane_count, -1)
    return (
        query_out,
        key_home.reshape(1, rounds, 1, -1),
        input_grad.reshape(1, rounds, 1, -1),
        ewc_grad,
    )


def solution(mesh):
    return jax.shard_map(
        body,
        mesh=mesh,
        in_specs=(
            P("fsdp", None, "seq", None),
            P("fsdp", None, "seq", None),
            P("fsdp", None, "seq", None),
            P("fsdp", None, "seq", None),
            P(("seq", "fsdp"), None),
            P(("seq", "fsdp"), None),
            P(("seq", "fsdp"), None),
            P("fsdp", None),
            P("fsdp", None),
        ),
        out_specs=(
            P("fsdp", "seq", None, None, None),
            P("fsdp", None, "seq", None),
            P("fsdp", None, "seq", None),
            P(("seq", "fsdp"), None),
        ),
        check_vma=False,
    )
```

profile of v0, /device:TPU:0, one launch (start us, length us, event | category | flops | bytes accessed | tf_op | source)
XLA Modules:
  0.0 2140.9 jit_solution(14226648482565059061)
XLA Ops:
  10.8 5.6 gather_fusion.4
  16.4 2.7 gather_fusion.2
  19.1 3.9 broadcast_select_fusion
  23.0 2.9 reshape.287
  25.9 3.9 reshape.283
  29.8 3.6 copy_select_fusion
  33.4 50.5 %all_to_all.30 = bf16[6,32,4,1024]{3,2,0,1:T(4,128)(2,1)} all-to-all(bf16[6,32,4,1024]{3,2,0,1:T(4,128)(2,1)S(1)} %get-tuple-element.56), channel_id=1, replica_groups=mesh['seq'=32,'fsdp'=8] {'seq'}, dimensions={1} | all-to-all | bytes 3145728 | tf_op jit(solution)/shard_map/all_to_all | solution.py:121
  83.9 5.5 all-to-all-start.3
  93.0 6.2 fusion.106
  103.4 640.9 %all-gather.2.cloned.1.call-done = bf16[4096,512]{1,0:T(8,128)(2,1)} async-done(((bf16[16,512]{1,0:T(8,128)(2,1)}), bf16[4096,512]{1,0:T(8,128)(2,1)}) %all-gather.2.cloned.1.call-update) | async-done | bytes 4194320 | tf_op jit(solution)/shard_map/all_gather | solution.py:84
  744.3 2.9 convolution_convert_fusion.9
  749.5 34.9 %all-to-all-start = ((bf16[6,32,4,128]{3,2,0,1:T(4,128)(2,1)}), bf16[6,32,4,128]{3,2,0,1:T(4,128)(2,1)S(1)}, u32[]{:S(2)}, u32[]{:S(2)}) async-start(bf16[6,32,4,128]{3,2,0,1:T(4,128)(2,1)} %get-tuple-element.58), calls=%async_computation | async-start | bytes 393216 | tf_op jit(solution)/shard_map/all_to_all | solution.py:123
  784.4 2.3 fusion.105
  790.3 6.1 all-to-all-done
  796.8 1.8 fusion.115
  800.5 1.8 fusion.112
  804.4 1.8 fusion.109
  808.0 1.8 fusion.118
  812.7 3.9 all-to-all-start.5
  816.7 11.8 all-to-all-done.5
  829.5 4.6 convolution_bitcast_fusion
  834.1 9.1 copy.468
  844.3 4.0 all-to-all-start.2
  849.5 10.8 all-to-all-done.2
  865.2 1.9 stack_reshape.37
  867.1 1.7 fusion.42
  872.1 1.7 fusion.43
  882.5 4.2 all-to-all-start.4
  889.1 2.4 reshape.288
  891.4 7.5 all-to-all-done.4
  900.8 4.7 fusion.4
  905.4 1227.0 %reduce-scatter.4.cloned.1.call-done = f32[16,512]{1,0:T(8,128)} async-done(((f32[4096,512]{1,0:T(8,128)}), f32[16,512]{1,0:T(8,128)}) %reduce-scatter.4.cloned.1.call-update) | async-done | bytes 32784 | tf_op jit(solution)/shard_map/reduce_scatter | solution.py:140
  (247 shorter events, 51.0 us)
Async XLA Ops:
  7.2 737.2 %copy-start = (bf16[1,128,1,4096]{3,1,2,0:T(8,128)(2,1)S(1)}, bf16[1,128,1,4096]{3,1,2,0:T(8,128)(2,1)}, u32[]{:S(2)}) copy-start(bf16[1,128,1,4096]{3,1,2,0:T(8,128)(2,1)} %param.15) | copy-start | bytes 3145732
  7.2 737.1 %all-gather.2.cloned.1.call-start = ((), (), s32[]{:S(2)}) async-start(), calls=%async_computation.7 | async-start | bytes 4210688 | tf_op jit(solution)/shard_map/all_gather | solution.py:84
  10.7 5.7 copy-start.2
  83.9 7.3 copy-start.3
  83.9 665.6 %all-to-all-start.3 = ((bf16[6,32,4,1024]{3,2,0,1:T(4,128)(2,1)}), bf16[6,32,4,1024]{3,2,0,1:T(4,128)(2,1)S(1)}, u32[]{:S(2)}, u32[]{:S(2)}) async-start(bf16[6,32,4,1024]{3,2,0,1:T(4,128)(2,1)} %get-tuple-element.55), calls=%async_computation.3 | async-start | bytes 3145728 | tf_op jit(solution)/shard_map/all_to_all | solution.py:122
  749.5 46.9 %all-to-all-start = ((bf16[6,32,4,128]{3,2,0,1:T(4,128)(2,1)}), bf16[6,32,4,128]{3,2,0,1:T(4,128)(2,1)S(1)}, u32[]{:S(2)}, u32[]{:S(2)}) async-start(bf16[6,32,4,128]{3,2,0,1:T(4,128)(2,1)} %get-tuple-element.58), calls=%async_computation | async-start | bytes 393216 | tf_op jit(solution)/shard_map/all_to_all | solution.py:123
  787.1 23.0 %copy-start.21 = (bf16[24,8,8,128]{3,2,1,0:T(8,128)(2,1)}, bf16[24,8,8,128]{3,2,1,0:T(8,128)(2,1)S(1)}, u32[]{:S(2)}) copy-start(bf16[24,8,8,128]{3,2,1,0:T(8,128)(2,1)S(1)} %copy.471) | copy-start | bytes 1179652
  789.2 7.6 copy-start.48
  796.7 11.3 copy-start.37
  796.7 7.6 copy-start.39
  796.8 3.8 copy-start.41
  810.0 6.6 copy-start.59
  810.0 6.6 copy-start.61
  812.7 15.8 all-to-all-start.5
  816.6 1315.8 %reduce-scatter.4.cloned.1.call-start = ((), (), s32[]{:S(2)}) async-start(), calls=%async_computation.8 | async-start | bytes 8421376 | tf_op jit(solution)/shard_map/reduce_scatter | solution.py:140
  816.6 17.4 copy-start.55
  816.7 17.4 copy-start.57
  844.1 4.3 copy-start.24
  844.3 16.0 all-to-all-start.2
  849.5 12.7 copy-start.52
  861.2 12.7 copy-start.46
  864.1 4.8 copy-start.9
  872.0 2.6 copy-start.15
  872.1 2.6 copy-start.25
  880.9 5.8 copy-start.38
  882.5 5.2 copy-start.20
  882.5 16.5 all-to-all-start.4
  891.4 8.6 copy-start.56
  900.0 1233.8 %copy-start.1 = (bf16[1,128,1,4096]{3,1,2,0:T(8,128)(2,1)S(1)}, bf16[1,128,1,4096]{3,1,2,0:T(8,128)(2,1)}, u32[]{:S(2)}) copy-start(bf16[1,128,1,4096]{3,1,2,0:T(8,128)(2,1)} %param.15) | copy-start | bytes 3145732
  900.8 1231.6 %copy-start.47 = (bf16[16,512]{1,0:T(8,128)(2,1)S(1)}, bf16[16,512]{1,0:T(8,128)(2,1)}, u32[]{:S(2)}) copy-start(bf16[16,512]{1,0:T(8,128)(2,1)} %param.19) | copy-start | bytes 49156
  900.8 1231.6 %copy-start.53 = (f32[16,512]{1,0:T(8,128)S(1)}, f32[16,512]{1,0:T(8,128)}, u32[]{:S(2)}) copy-start(f32[16,512]{1,0:T(8,128)} %param.21) | copy-start | bytes 98308
  900.8 1231.6 %copy-start.54 = (f32[16,512]{1,0:T(8,128)S(1)}, f32[16,512]{1,0:T(8,128)}, u32[]{:S(2)}) copy-start(f32[16,512]{1,0:T(8,128)} %param.20) | copy-start | bytes 98308
  (37 other events, 57.2 us)
Sparse Core Ops, SparseCore 0:
  9.9 734.4 all-gather.1
  843.3 1289.0 reduce-scatter.3
where the time goes:
time: 2150 us; the launch traced here: 2140 us
  waiting for transfers between devices  1900 us (88%)
  local copies, waits for them, and re-layouts  65.1 us (3%)
  starting transfers between devices  52.6 us (2%)
  blocking collectives  50.5 us (2%)
  matrix products  33.8 us (2%)
    reduce_scatter x1, waiting for transfers between devices, body(): lax.psum_scatter(partial_sum, ('seq', 'fsdp'), scatter_dimension=0, tiled...  1230 us
    all_gather x1, waiting for transfers between devices, fetch_weight(): return lax.all_gather(value_weight, ('seq', 'fsdp'), axis=0, tiled=True)  641 us
    all_to_all x1, blocking collectives, body(): lax.all_to_all(query_send, 'seq', split_axis=1, concat_axis=1, tiled=True)  50.5 us
  transfers between devices with their start and end apart: 7, of which 6 were waited for; matrix products, arithmetic and copies ran while one was open for 4% of the time, Pallas kernels for 0%

commit v1 on v0

--- a/solution.py
+++ b/solution.py
@@ -3,6 +3,7 @@
 import jax.numpy as jnp
 from jax import lax
 from jax.sharding import PartitionSpec as P
+from jax.lax import all_to_all, axis_size
 
 KVH = 4
 HD = 128
@@ -81,7 +82,19 @@
 
 
 def fetch_weight(value_weight):
-    return lax.all_gather(value_weight, ("seq", "fsdp"), axis=0, tiled=True)
+
+    def _connect_orders(panel):
+        return jnp.concatenate(
+            all_to_all(
+                jnp.stack([panel] * axis_size(("seq", "fsdp"))),
+                split_axis=0,
+                axis_name=("seq", "fsdp"),
+                concat_axis=0,
+            ),
+            axis=0,
+        )
+
+    return _connect_orders(value_weight)
 
 
 def body(inputs, queries, rotated_keys, out_grad, value_weight, fisher, anchor, doc_starts, owners):

time: 2150 us -> 1610 us (0.75)
  waiting for transfers between devices: 1900 us -> 1290 us
  blocking collectives: 50.5 us -> 157 us
  starting transfers between devices: 52.6 us -> 21.8 us
    all_gather x1 -> x0, waiting for transfers between devices: 641 us -> none  [fetch_weight(): return lax.all_gather(value_weight, ('seq', 'fsdp'), axis=0, tiled=True)]
    all_to_all x0 -> x1, blocking collectives: none -> 108 us  [_connect_orders(): all_to_all(jnp.stack([panel] * axis_size(('seq', 'fsdp'))), split_axis=0,...]
    all_to_all x1, starting transfers between devices: 34.9 us -> 4.95 us  [body(): lax.all_to_all(key_send, 'seq', split_axis=1, concat_axis=1, tiled=True)]
    all_to_all x1, waiting for transfers between devices: 0.01 us -> 23.4 us  [body(): lax.all_to_all(grad_send, 'seq', split_axis=1, concat_axis=1, tiled=True)]
  transfers between devices with their start and end apart: 7 -> 6, of which waited for: 6 -> 6; matrix products, arithmetic and copies ran while one was open for 4% -> 3% of each run, Pallas kernels for 0% -> 0%
where the time goes in v1:
time: 1610 us; the launch traced here: 1600 us
  waiting for transfers between devices  1290 us (80%)
  blocking collectives  157 us (10%)
  local copies, waits for them, and re-layouts  65.4 us (4%)
  matrix products  31.7 us (2%)
  starting transfers between devices  21.8 us (1%)
  other arithmetic  18.7 us (1%)
    reduce_scatter x1, waiting for transfers between devices, body(): lax.psum_scatter(partial_sum, ('seq', 'fsdp'), scatter_dimension=0, tiled...  1230 us
    all_to_all x1, blocking collectives, _connect_orders(): all_to_all(jnp.stack([panel] * axis_size(('seq', 'fsdp'))), split_axis=0,...  108 us
    all_to_all x1, blocking collectives, body(): lax.all_to_all(query_send, 'seq', split_axis=1, concat_axis=1, tiled=True)  49.4 us
  transfers between devices with their start and end apart: 6, of which 6 were waited for; matrix products, arithmetic and copies ran while one was open for 3% of the time, Pallas kernels for 0%

profile of v1, /device:TPU:0, one launch (start us, length us, event | category | flops | bytes accessed | tf_op | source)
XLA Modules:
  0.0 1599.4 jit_solution(2326362195158197606)
XLA Ops:
  9.9 5.6 gather_fusion.4
  15.5 2.7 gather_fusion.2
  18.2 3.9 broadcast_select_fusion
  22.1 2.9 reshape.293
  25.0 3.9 reshape.288
  28.9 3.6 copy_select_fusion
  32.5 49.4 %all_to_all.35 = bf16[6,32,4,1024]{3,2,0,1:T(4,128)(2,1)} all-to-all(bf16[6,32,4,1024]{3,2,0,1:T(4,128)(2,1)S(1)} %get-tuple-element.56), channel_id=1, replica_groups=mesh['seq'=32,'fsdp'=8] {'seq'}, dimensions={1} | all-to-all | bytes 3145728 | tf_op jit(solution)/shard_map/all_to_all | solution.py:134
  82.4 107.7 %all_to_all.36 = bf16[256,16,512]{2,1,0:T(8,128)(2,1)} all-to-all(bf16[256,16,512]{2,1,0:T(8,128)(2,1)S(1)} %stack.8), channel_id=1, replica_groups=mesh['seq'=32,'fsdp'=8] {'seq','fsdp'}, dimensions={0} | all-to-all | bytes 8388608 | tf_op jit(solution)/shard_map/all_to_all | solution.py:88
  190.1 4.6 all-to-all-start.4
  198.3 6.2 fusion.106
  211.8 23.4 %all-to-all-done.4 = bf16[6,32,4,1024]{3,2,0,1:T(4,128)(2,1)S(1)} async-done(((bf16[6,32,4,1024]{3,2,0,1:T(4,128)(2,1)}), bf16[6,32,4,1024]{3,2,0,1:T(4,128)(2,1)S(1)}, u32[]{:S(2)}, u32[]{:S(2)}) %all-to-all-start.4) | async-done | bytes 1572896 | tf_op jit(solution)/shard_map/all_to_all | solution.py:135
  235.2 5.0 all-to-all-start
  240.2 2.3 fusion.105
  246.0 6.5 all-to-all-done
  252.9 1.8 fusion.115
  256.7 1.8 fusion.112
  260.5 1.8 fusion.109
  264.2 1.8 fusion.118
  268.8 3.9 all-to-all-start.6
  272.8 11.8 all-to-all-done.6
  285.6 4.6 convolution_bitcast_fusion
  290.1 9.1 copy.468
  300.4 4.1 all-to-all-start.3
  305.6 10.5 all-to-all-done.3
  321.0 1.9 stack_reshape.37
  322.9 1.7 fusion.42
  327.9 1.7 fusion.43
  338.3 4.2 all-to-all-start.5
  344.9 2.4 reshape.294
  347.3 8.1 all-to-all-done.5
  357.2 4.7 fusion.4
  361.9 1229.0 %reduce-scatter.4.cloned.1.call-done = f32[16,512]{1,0:T(8,128)} async-done(((f32[4096,512]{1,0:T(8,128)}), f32[16,512]{1,0:T(8,128)}) %reduce-scatter.4.cloned.1.call-update) | async-done | bytes 32784 | tf_op jit(solution)/shard_map/reduce_scatter | solution.py:153
  (250 shorter events, 51.4 us)
Async XLA Ops:
  7.2 201.6 %copy-start = (bf16[1,128,1,4096]{3,1,2,0:T(8,128)(2,1)S(1)}, bf16[1,128,1,4096]{3,1,2,0:T(8,128)(2,1)}, u32[]{:S(2)}) copy-start(bf16[1,128,1,4096]{3,1,2,0:T(8,128)(2,1)} %param.15) | copy-start | bytes 3145732
  9.9 5.6 copy-start.2
  32.5 49.4 %copy-start.48 = (bf16[16,512]{1,0:T(8,128)(2,1)S(1)}, bf16[16,512]{1,0:T(8,128)(2,1)}, u32[]{:S(2)}) copy-start(bf16[16,512]{1,0:T(8,128)(2,1)} %param.19) | copy-start | bytes 49156
  190.1 6.5 copy-start.4
  190.1 45.1 %all-to-all-start.4 = ((bf16[6,32,4,1024]{3,2,0,1:T(4,128)(2,1)}), bf16[6,32,4,1024]{3,2,0,1:T(4,128)(2,1)S(1)}, u32[]{:S(2)}, u32[]{:S(2)}) async-start(bf16[6,32,4,1024]{3,2,0,1:T(4,128)(2,1)} %get-tuple-element.55), calls=%async_computation.4 | async-start | bytes 3145728 | tf_op jit(solution)/shard_map/all_to_all | solution.py:135
  205.8 2.9 copy-start.3
  235.2 17.3 %all-to-all-start = ((bf16[6,32,4,128]{3,2,0,1:T(4,128)(2,1)}), bf16[6,32,4,128]{3,2,0,1:T(4,128)(2,1)S(1)}, u32[]{:S(2)}, u32[]{:S(2)}) async-start(bf16[6,32,4,128]{3,2,0,1:T(4,128)(2,1)} %get-tuple-element.58), calls=%async_computation | async-start | bytes 393216 | tf_op jit(solution)/shard_map/all_to_all | solution.py:136
  242.8 23.4 %copy-start.22 = (bf16[24,8,8,128]{3,2,1,0:T(8,128)(2,1)}, bf16[24,8,8,128]{3,2,1,0:T(8,128)(2,1)S(1)}, u32[]{:S(2)}) copy-start(bf16[24,8,8,128]{3,2,1,0:T(8,128)(2,1)S(1)} %copy.471) | copy-start | bytes 1179652
  244.9 8.0 copy-start.50
  252.8 11.3 copy-start.38
  252.8 7.6 copy-start.40
  252.9 3.8 copy-start.42
  266.1 6.6 copy-start.61
  266.2 6.6 copy-start.63
  268.8 15.8 all-to-all-start.6
  272.7 1318.2 %reduce-scatter.4.cloned.1.call-start = ((), (), s32[]{:S(2)}) async-start(), calls=%async_computation.8 | async-start | bytes 8421376 | tf_op jit(solution)/shard_map/reduce_scatter | solution.py:153
  272.8 17.4 %copy-start.57 = (pred[128]{0:T(512)(128)(4,1)}, pred[128]{0:T(512)(128)(4,1)S(1)}, u32[]{:S(2)}) copy-start(pred[128]{0:T(512)(128)(4,1)S(1)} %get-tuple-element.37) | copy-start | bytes 388
  272.8 17.4 %copy-start.59 = (s32[1024]{0:T(1024)}, s32[1024]{0:T(1024)S(1)}, u32[]{:S(2)}) copy-start(s32[1024]{0:T(1024)S(1)} %pad_clamp_fusion) | copy-start | bytes 12292
  300.2 4.3 copy-start.25
  300.4 15.7 all-to-all-start.3
  305.6 12.4 copy-start.54
  317.0 12.7 copy-start.47
  319.9 4.8 copy-start.10
  327.9 2.6 copy-start.16
  336.7 5.9 copy-start.39
  338.3 5.2 copy-start.21
  338.3 17.1 %all-to-all-start.5 = ((bf16[6,32,4,128]{3,2,0,1:T(4,128)(2,1)}), bf16[6,32,4,128]{3,2,0,1:T(4,128)(2,1)S(1)}, u32[]{:S(2)}, u32[]{:S(2)}) async-start(bf16[6,32,4,128]{3,2,0,1:T(4,128)(2,1)} %pad_maximum_fusion.1), calls=%async_computation.5 | async-start | bytes 393216 | tf_op jit(solution)/shard_map/all_to_all | solution.py:141
  347.3 9.2 copy-start.58
  356.5 1235.8 %copy-start.1 = (bf16[1,128,1,4096]{3,1,2,0:T(8,128)(2,1)S(1)}, bf16[1,128,1,4096]{3,1,2,0:T(8,128)(2,1)}, u32[]{:S(2)}) copy-start(bf16[1,128,1,4096]{3,1,2,0:T(8,128)(2,1)} %param.15) | copy-start | bytes 3145732
  357.2 1233.6 %copy-start.49 = (bf16[16,512]{1,0:T(8,128)(2,1)S(1)}, bf16[16,512]{1,0:T(8,128)(2,1)}, u32[]{:S(2)}) copy-start(bf16[16,512]{1,0:T(8,128)(2,1)} %param.19) | copy-start | bytes 49156
  357.2 1233.6 %copy-start.55 = (f32[16,512]{1,0:T(8,128)S(1)}, f32[16,512]{1,0:T(8,128)}, u32[]{:S(2)}) copy-start(f32[16,512]{1,0:T(8,128)} %param.21) | copy-start | bytes 98308
  357.2 1233.6 %copy-start.56 = (f32[16,512]{1,0:T(8,128)S(1)}, f32[16,512]{1,0:T(8,128)}, u32[]{:S(2)}) copy-start(f32[16,512]{1,0:T(8,128)} %param.20) | copy-start | bytes 98308
  (38 other events, 59.5 us)
Sparse Core Ops, SparseCore 0:
  299.3 1291.4 reduce-scatter.3
